TPU v7x, 32 devices: a whole 2x2x4 slice. The times are simulated.
32 devices in a mesh: groups: 2 (over y), role: 4 (over x, core), tp: 4 (over z).
Axes of the slice: x: 2, y: 2, z: 4, core: 2. Of those that a mesh axis runs over, the one named last changes fastest.
Arguments:
- x_teacher: bfloat16 [512, 8192], P('groups', 'tp'), parts along dimension 0, may hold values from -6 to 6
- x_student: bfloat16 [512, 4096], P('groups', 'role'), parts along dimension 0, may hold values from -6 to 6
- t_gate: bfloat16 [8192, 14336], P('tp', 'role'), may hold values from -0.0625 to 0.0625
- t_up: bfloat16 [8192, 14336], P('tp', 'role'), may hold values from -0.0625 to 0.0625
- t_down: bfloat16 [14336, 8192], P('role', 'tp'), may hold values from -0.046875 to 0.046875
- s_gate: bfloat16 [4096, 8192], P('role', 'tp'), may hold values from -0.09375 to 0.09375
- s_up: bfloat16 [4096, 8192], P('role', 'tp'), may hold values from -0.09375 to 0.09375
- s_down: bfloat16 [8192, 4096], P('tp', 'role'), may hold values from -0.0625 to 0.0625
- align: bfloat16 [4096, 8192], P('role', 'tp'), may hold values from -0.09375 to 0.09375
Outputs:
- grad_s_gate: bfloat16 [8192, 8192], P(('groups', 'role'), 'tp'), parts along dimension 0
- grad_s_up: bfloat16 [8192, 8192], P(('groups', 'role'), 'tp'), parts along dimension 0
- grad_s_down: bfloat16 [16384, 4096], P(('groups', 'tp'), 'role'), parts along dimension 0
- grad_align: bfloat16 [8192, 8192], P(('groups', 'role'), 'tp'), parts along dimension 0
There are 2 independent parts, one for each index of `groups`. A program takes and returns all parts, laid end to end along the dimension named above; an argument that names none is the same for every part. Nothing has to cross between parts.
All inputs are finite; a program needn't handle non-finite values.
Results may differ from a plain program's by a relative error of at most 0.009.
Values may be sent and summed in bfloat16 or wider, within the bound.
No kernel may reach another device: no remote copies, remote signals or barrier semaphores. Data moves between devices by JAX's collectives and lax.ppermute only.
A program may use at most 128 MiB of HBM per device.

v0:
```python
import jax
import jax.numpy as jnp
from jax import lax
from jax.sharding import PartitionSpec as P

loss_scale = 16.0


def contract_rows(left, right):
    return lax.dot_general(
        left, right, (((0,), (0,)), ((), ())), preferred_element_type=jnp.float32
    )


def contract_cols(left, right):
    return lax.dot_general(
        left, right, (((1,), (1,)), ((), ())), preferred_element_type=jnp.float32
    )


def role_sums(values):
    return lax.psum(values, "role")


def tp_sums(values):
    return lax.psum(values, "tp")


def tp_scatter(term_fn, share_rows):
    return lax.psum_scatter(
        term_fn(jnp.int32(0), lax.axis_size("tp") * share_rows),
        "tp",
        scatter_dimension=0,
        tiled=True,
    )


def tp_gather(shares, piece_fn):
    return piece_fn(lax.all_gather(shares, "tp", axis=0, tiled=True), jnp.int32(0))


def on_device(x_teacher, x_student, t_gate, t_up, t_down, s_gate, s_up, s_down, align):
    token_count = x_teacher.shape[0]
    unit_count = t_gate.shape[1]
    tp_devices = lax.axis_size("tp")

    def token_term(first_row, row_count):
        gate_rows = jnp.dot(x_teacher, t_gate, preferred_element_type=jnp.float32)
        up_rows = jnp.dot(x_teacher, t_up, preferred_element_type=jnp.float32)
        return jnp.concatenate([gate_rows, up_rows], axis=1)

    def project_rows(part_rows, first_row):
        return jnp.dot(part_rows, t_down, preferred_element_type=jnp.float32)

    shares = tp_scatter(token_term, token_count // tp_devices)
    hidden_share = (jax.nn.silu(shares[:, :unit_count]) * shares[:, unit_count:]).astype(
        jnp.bfloat16
    )
    features_part = tp_gather(hidden_share, project_rows)
    student_gate_part = jnp.dot(x_student, s_gate, preferred_element_type=jnp.float32)
    student_up_part = jnp.dot(x_student, s_up, preferred_element_type=jnp.float32)
    student_gate, student_up = role_sums((student_gate_part, student_up_part))
    gate_sigmoid = jax.nn.sigmoid(student_gate)
    gate_active = student_gate * gate_sigmoid
    student_hidden = (gate_active * student_up).astype(jnp.bfloat16)
    student_out = tp_sums(
        jnp.dot(student_hidden, s_down, preferred_element_type=jnp.float32)
    ).astype(jnp.bfloat16)
    aligned_part = jnp.dot(student_out, align, preferred_element_type=jnp.float32)
    difference = role_sums(aligned_part - features_part)
    grad_aligned = (difference * (2.0 * loss_scale / token_count)).astype(jnp.bfloat16)
    grad_align = contract_rows(student_out, grad_aligned).astype(jnp.bfloat16)
    grad_student_out = tp_sums(contract_cols(grad_aligned, align)).astype(jnp.bfloat16)
    grad_s_down = contract_rows(student_hidden, grad_student_out).astype(jnp.bfloat16)
    grad_hidden = role_sums(contract_cols(grad_student_out, s_down))
    slope = gate_sigmoid * (1.0 + student_gate * (1.0 - gate_sigmoid))
    grad_gate_pre = (grad_hidden * student_up * slope).astype(jnp.bfloat16)
    grad_up_pre = (grad_hidden * gate_active).astype(jnp.bfloat16)
    grad_s_gate = contract_rows(x_student, grad_gate_pre).astype(jnp.bfloat16)
    grad_s_up = contract_rows(x_student, grad_up_pre).astype(jnp.bfloat16)
    return (grad_s_gate, grad_s_up, grad_s_down, grad_align)


def solution(mesh):
    placed = (
        P("groups", "tp"),
        P("groups", "role"),
        P("tp", "role"),
        P("tp", "role"),
        P("role", "tp"),
        P("role", "tp"),
        P("role", "tp"),
        P("tp", "role"),
        P("role", "tp"),
    )
    return jax.shard_map(
        on_device,
        mesh=mesh,
        in_specs=placed,
        out_specs=(
            P(("groups", "role"), "tp"),
            P(("groups", "role"), "tp"),
            P(("groups", "tp"), "role"),
            P(("groups", "role"), "tp"),
        ),
        check_vma=False,
    )
```

profile of v0, /device:TPU:0, one launch (start us, length us, event | category | flops | bytes accessed | tf_op | source)
XLA Modules:
  0.0 431.9 jit_solution(6002679710210174196)
XLA Ops:
  8.0 0.0 copy-start
  8.0 0.0 reduce-scatter.2.cloned.1.call-start
  8.1 1.2 copy-done
  9.2 7.2 %fusion.18 = f32[256,3584]{1,0:T(8,128)S(1)} fusion(bf16[256,2048]{1,0:T(8,128)(2,1)S(1)} %copy-done, bf16[2048,3584]{1,0:T(8,128)(2,1)} %param.12), kind=kOutput, calls=%fused_computation.29 | convolution fusion | flops 3758096384 | bytes 19398656 | tf_op jit(solution)/shard_map/dot_general | solution.py:49
  16.5 7.3 %fusion.17 = f32[256,3584]{1,0:T(8,128)S(1)} fusion(bf16[256,2048]{1,0:T(8,128)(2,1)S(1)} %copy-done, bf16[2048,3584]{1,0:T(8,128)(2,1)} %param.11), kind=kOutput, calls=%fused_computation.28 | convolution fusion | flops 3758096384 | bytes 19398656 | tf_op jit(solution)/shard_map/dot_general | solution.py:48
  23.8 3.4 pad_maximum_fusion
  27.2 0.0 copy-start.7
  27.2 0.0 reduce-scatter.2.cloned.1.call-update
  27.3 0.0 all-reduce.11.cloned.1.call-start
  27.3 1.0 copy-done.7
  28.3 0.0 copy-start.5
  28.3 4.9 %fusion.14 = f32[256,2048]{1,0:T(8,128)} fusion(bf16[256,1024]{1,0:T(8,128)(2,1)S(1)} %copy-done.7, bf16[1024,2048]{1,0:T(8,128)(2,1)} %param.14), kind=kOutput, calls=%fused_computation.25 | convolution fusion | flops 1073741824 | bytes 6815744 | tf_op jit(solution)/shard_map/dot_general | solution.py:60
  33.2 0.0 copy-done.5
  33.2 2.6 fusion.15
  35.8 0.0 all-reduce.11.cloned.1.call-update
  35.8 0.0 all-gather.2.cloned.1.call-start
  35.9 122.1 %reduce-scatter.2.cloned.1.call-done = f32[64,7168]{1,0:T(8,128)} async-done(((f32[256,7168]{1,0:T(8,128)}), f32[64,7168]{1,0:T(8,128)}) %reduce-scatter.2.cloned.1.call-update) | async-done | bytes 1835024 | tf_op jit(solution)/shard_map/reduce_scatter | solution.py:30
  158.0 2.5 fusion.2
  160.4 0.0 all-gather.2.cloned.1.call-update
  160.5 0.0 all-reduce.7.cloned.1.call-start
  160.5 0.0 all-reduce.11.cloned.1.call-done
  160.5 0.0 copy-start.6
  160.6 3.0 multiply_convert_fusion.3
  163.5 0.5 copy-done.6
  164.0 1.3 fusion.16
  165.3 69.8 %all-reduce.12 = bf16[256,1024]{1,0:T(8,128)(2,1)S(1)} all-reduce(f32[256,1024]{1,0:T(8,128)S(1)} %fusion.16), channel_id=1, replica_groups=mesh['groups'=2,'role'=4,'tp'=4] {'tp'}, use_global_device_ids=true, to_apply=%region_2.3 | all-reduce | flops 262144 | bytes 1572864 | tf_op jit(solution)/shard_map/psum | solution.py:26
  235.0 0.0 all-gather.2.cloned.1.call-done
  235.1 0.0 copy-start.2
  235.1 7.9 %fusion.19 = f32[256,2048]{1,0:T(8,128)S(1)} fusion(bf16[256,3584]{1,0:T(8,128)(2,1)} %all-gather.2.cloned.1.call-done, bf16[3584,2048]{1,0:T(8,128)(2,1)} %param.13), kind=kOutput, calls=%fused_computation.30 | convolution fusion | flops 3758096384 | bytes 18612224 | tf_op jit(solution)/shard_map/dot_general | solution.py:53
  243.0 0.0 copy-done.2
  243.0 2.6 convolution_subtract_fusion
  245.7 0.0 all-reduce.7.cloned.1.call-update
  245.7 0.2 all-reduce.9.cloned.1.call-start
  245.9 51.1 %all-reduce.7.cloned.1.call-done = f32[256,2048]{1,0:T(8,128)} async-done(((f32[256,2048]{1,0:T(8,128)}), f32[256,2048]{1,0:T(8,128)}) %all-reduce.7.cloned.1.call-update) | async-done | bytes 2097168 | tf_op jit(solution)/shard_map/psum | solution.py:22
  297.0 4.1 fusion.3
  301.2 43.6 %all-reduce.13 = bf16[256,1024]{1,0:T(8,128)(2,1)S(1)} all-reduce(f32[256,1024]{1,0:T(8,128)S(1)} %fusion.3), channel_id=1, replica_groups=mesh['groups'=2,'role'=4,'tp'=4] {'tp'}, use_global_device_ids=true, to_apply=%region_5.6 | all-reduce | flops 262144 | bytes 1572864 | tf_op jit(solution)/shard_map/psum | solution.py:26
  344.8 4.8 %fusion.20 = f32[256,2048]{1,0:T(8,128)} fusion(bf16[256,1024]{1,0:T(8,128)(2,1)S(1)} %all-reduce.13, bf16[2048,1024]{1,0:T(8,128)(2,1)} %param.16), kind=kOutput, calls=%fused_computation.31 | convolution fusion | flops 1073741824 | bytes 6815744 | tf_op jit(solution)/shard_map/dot_general | solution.py:16
  349.6 0.0 all-reduce.9.cloned.1.call-update
  349.6 0.0 copy-start.3
  349.6 3.3 convolution_convert_fusion.1
  352.9 0.0 copy-done.3
  352.9 0.0 copy-start.8
  352.9 3.3 convolution_convert_fusion
  356.2 43.1 %all-reduce.9.cloned.1.call-done = f32[256,2048]{1,0:T(8,128)} async-done(((f32[256,2048]{1,0:T(8,128)}), f32[256,2048]{1,0:T(8,128)}) %all-reduce.9.cloned.1.call-update) | async-done | bytes 2097168 | tf_op jit(solution)/shard_map/psum | solution.py:22
  399.3 0.0 copy-done.8
  399.3 7.0 %convert_bitcast_fusion.1 = bf16[1024,2048]{0,1:T(8,128)(2,1)} fusion(bf16[256,1024]{1,0:T(8,128)(2,1)S(1)} %copy-done.8, f32[256,2048]{1,0:T(8,128)} %get-tuple-element.8, f32[256,2048]{1,0:T(8,128)} %all-reduce.9.cloned.1.call-done, f32[256,2048]{1,0:T(8,128)} %get-tuple-element.9), kind=kOutput, calls=%fused_computation.2 | convolution fusion | flops 1081081856 | bytes 11010048 | tf_op jit(solution)/shard_map/dot_general | solution.py:10
  406.3 0.0 copy-start.4
  406.3 6.6 %copy.13 = bf16[1024,2048]{1,0:T(8,128)(2,1)} copy(bf16[1024,2048]{0,1:T(8,128)(2,1)} %convert_bitcast_fusion.1) | data formatting | bytes 8388608
  412.9 0.0 copy-done.4
  412.9 4.9 %convert_bitcast_fusion = bf16[1024,2048]{0,1:T(8,128)(2,1)} fusion(bf16[256,1024]{1,0:T(8,128)(2,1)S(1)} %copy-done.8, f32[256,2048]{1,0:T(8,128)} %all-reduce.9.cloned.1.call-done, f32[256,2048]{1,0:T(8,128)S(1)} %copy-done.4), kind=kOutput, calls=%fused_computation.1 | convolution fusion | flops 1078984704 | bytes 8912896 | tf_op jit(solution)/shard_map/dot_general | solution.py:10
  417.8 0.0 copy-start.1
  417.8 6.5 %copy.14 = bf16[1024,2048]{1,0:T(8,128)(2,1)} copy(bf16[1024,2048]{0,1:T(8,128)(2,1)} %convert_bitcast_fusion) | data formatting | bytes 8388608
  424.3 0.0 copy-done.1
Async XLA Ops:
  8.0 1.2 copy-start
  8.0 150.0 %reduce-scatter.2.cloned.1.call-start = ((), (), s32[]{:S(2)}) async-start(), calls=%async_computation.1 | async-start | bytes 9175040 | tf_op jit(solution)/shard_map/reduce_scatter | solution.py:30
  27.2 1.0 copy-start.7
  27.3 133.3 %all-reduce.11.cloned.1.call-start = ((), (), s32[]{:S(2)}) async-start(), calls=%async_computation.5 | async-start | bytes 8388608 | tf_op jit(solution)/shard_map/psum | solution.py:22
  28.3 4.9 %copy-start.5 = (bf16[1024,2048]{1,0:T(8,128)(2,1)S(1)}, bf16[1024,2048]{1,0:T(8,128)(2,1)}, u32[]{:S(2)}) copy-start(bf16[1024,2048]{1,0:T(8,128)(2,1)} %param.15) | copy-start | bytes 12582916
  35.8 199.2 %all-gather.2.cloned.1.call-start = ((), (), s32[]{:S(2)}) async-start(), calls=%async_computation.2 | async-start | bytes 2293760 | tf_op jit(solution)/shard_map/all_gather | solution.py:39
  160.5 136.6 %all-reduce.7.cloned.1.call-start = ((), (), s32[]{:S(2)}) async-start(), calls=%async_computation.3 | async-start | bytes 4194304 | tf_op jit(solution)/shard_map/psum | solution.py:22
  160.5 3.5 copy-start.6
  235.1 8.0 %copy-start.2 = (bf16[1024,2048]{1,0:T(8,128)(2,1)S(1)}, bf16[1024,2048]{1,0:T(8,128)(2,1)}, u32[]{:S(2)}) copy-start(bf16[1024,2048]{1,0:T(8,128)(2,1)} %param.17) | copy-start | bytes 12582916
  245.7 153.6 %all-reduce.9.cloned.1.call-start = ((), (), s32[]{:S(2)}) async-start(), calls=%async_computation.4 | async-start | bytes 4194304 | tf_op jit(solution)/shard_map/psum | solution.py:22
  349.6 3.3 copy-start.3
  352.9 46.4 %copy-start.8 = (bf16[256,1024]{1,0:T(8,128)(2,1)S(1)}, bf16[256,1024]{1,0:T(8,128)(2,1)}, u32[]{:S(2)}) copy-start(bf16[256,1024]{1,0:T(8,128)(2,1)} %param.10) | copy-start | bytes 1572868
  406.3 6.6 %copy-start.4 = (f32[256,2048]{1,0:T(8,128)S(1)}, f32[256,2048]{1,0:T(8,128)}, u32[]{:S(2)}) copy-start(f32[256,2048]{1,0:T(8,128)} %get-tuple-element.8) | copy-start | bytes 6291460
  417.8 6.5 %copy-start.1 = (bf16[256,2048]{1,0:T(8,128)(2,1)S(1)}, bf16[256,2048]{1,0:T(8,128)(2,1)}, u32[]{:S(2)}) copy-start(bf16[256,2048]{1,0:T(8,128)(2,1)} %param.9) | copy-start | bytes 3145732
Sparse Core Ops, SparseCore 0:
  27.4 130.5 reduce-scatter.1
  160.6 69.2 all-gather.1
Sparse Core Ops, SparseCore 1:
  35.9 88.1 all-reduce.10
  245.8 51.2 all-reduce.6
  349.7 49.6 all-reduce.8
where the time goes:
time: 432 us
  waiting for transfers between devices  216 us (50%)
  blocking collectives  113 us (26%)
  matrix products  61.3 us (14%)
  between operations  15.8 us (4%)
  local copies, waits for them, and re-layouts  15.7 us (4%)
  other arithmetic  8.9 us (2%)
    reduce_scatter x1, waiting for transfers between devices, tp_scatter(): lax.psum_scatter(term_fn(jnp.int32(0), lax.axis_size('tp') * share_rows),...  122 us
    psum x2, blocking collectives, tp_sums(): return lax.psum(values, 'tp')  113 us
    psum x3, waiting for transfers between devices, role_sums(): return lax.psum(values, 'role')  94.2 us
    dot_general x4, matrix products, contract_rows(): lax.dot_general(left, right, (((0,), (0,)), ((), ())), preferred_element_...  18.5 us
    unnamed x20, local copies, waits for them, and re-layouts  15.7 us
    dot_general x2, matrix products, contract_cols(): lax.dot_general(left, right, (((1,), (1,)), ((), ())), preferred_element_...  8.9 us
  transfers between devices with their start and end apart: 5, of which 3 were waited for; matrix products, arithmetic and copies ran while one was open for 5% of the time, Pallas kernels for 0%

commit v1 on v0

--- a/solution.py
+++ b/solution.py
@@ -23,7 +23,7 @@
 
 
 def tp_sums(values):
-    return lax.psum(values, "tp")
+    return jnp.sum(lax.all_gather(values, "tp"), axis=0)
 
 
 def tp_scatter(term_fn, share_rows):

time: 432 us -> 527 us (1.22)
  waiting for transfers between devices: 216 us -> 417 us
  blocking collectives: 113 us -> 0 us
  other arithmetic: 8.9 us -> 14.3 us
    all_gather x0 -> x2, waiting for transfers between devices: none -> 161 us  [tp_sums(): return jnp.sum(lax.all_gather(values, 'tp'), axis=0)]
    psum x2 -> x0, blocking collectives: 113 us -> none  [tp_sums(): return lax.psum(values, 'tp')]
    reduce_scatter x1, waiting for transfers between devices: 122 us -> 54.5 us  [tp_scatter(): lax.psum_scatter(term_fn(jnp.int32(0), lax.axis_size('tp') * share_rows),...]
    psum x3, waiting for transfers between devices: 94.2 us -> 161 us  [role_sums(): return lax.psum(values, 'role')]
    all_gather x1, waiting for transfers between devices: 0.02 us -> 39 us  [tp_gather(): lax.all_gather(shares, 'tp', axis=0, tiled=True)]
    reduce_sum x0 -> x2, other arithmetic: none -> 5.39 us  [tp_sums(): return jnp.sum(lax.all_gather(values, 'tp'), axis=0)]
    unnamed x20 -> x18, local copies, waits for them, and re-layouts: 15.7 us -> 13.6 us
  transfers between devices with their start and end apart: 5 -> 7, of which waited for: 3 -> 7; matrix products, arithmetic and copies ran while one was open for 5% -> 7% of each run, Pallas kernels for 0% -> 0%
where the time goes in v1:
time: 527 us; the launch traced here: 526 us
  waiting for transfers between devices  417 us (79%)
  matrix products  65.7 us (12%)
  between operations  15.6 us (3%)
  other arithmetic  14.3 us (3%)
  local copies, waits for them, and re-layouts  13.6 us (3%)
    psum x3, waiting for transfers between devices, role_sums(): return lax.psum(values, 'role')  161 us
    all_gather x2, waiting for transfers between devices, tp_sums(): return jnp.sum(lax.all_gather(values, 'tp'), axis=0)  161 us
    reduce_scatter x1, waiting for transfers between devices, tp_scatter(): lax.psum_scatter(term_fn(jnp.int32(0), lax.axis_size('tp') * share_rows),...  54.5 us
    all_gather x1, waiting for transfers between devices, tp_gather(): lax.all_gather(shares, 'tp', axis=0, tiled=True)  39 us
    dot_general x4, matrix products, contract_rows(): lax.dot_general(left, right, (((0,), (0,)), ((), ())), preferred_element_...  20.1 us
    unnamed x18, local copies, waits for them, and re-layouts  13.6 us
  transfers between devices with their start and end apart: 7, of which 7 were waited for; matrix products, arithmetic and copies ran while one was open for 7% of the time, Pallas kernels for 0%

profile of v1, /device:TPU:0, one launch (start us, length us, event | category | flops | bytes accessed | tf_op | source)
XLA Modules:
  0.0 526.1 jit_solution(7959304496718467282)
XLA Ops:
  8.0 0.0 copy-start
  8.0 0.0 copy-start.6
  8.0 0.0 all-reduce.9.cloned.1.call-start
  8.1 0.0 copy-start.4
  8.1 5.1 fusion.14
  13.2 0.0 copy-done.6
  13.2 0.0 copy-done.4
  13.2 2.6 fusion.15
  15.8 0.0 all-reduce.9.cloned.1.call-update
  15.8 0.0 reduce-scatter.2.cloned.1.call-start
  15.8 0.0 copy-done
  15.9 7.3 %fusion.18 = f32[256,3584]{1,0:T(8,128)S(1)} fusion(bf16[256,2048]{1,0:T(8,128)(2,1)S(1)} %copy-done, bf16[2048,3584]{1,0:T(8,128)(2,1)} %param.12), kind=kOutput, calls=%fused_computation.29 | convolution fusion | flops 3758096384 | bytes 19398656 | tf_op jit(solution)/shard_map/dot_general | solution.py:49
  23.1 8.0 %fusion.17 = f32[256,3584]{1,0:T(8,128)S(1)} fusion(bf16[256,2048]{1,0:T(8,128)(2,1)S(1)} %copy-done, bf16[2048,3584]{1,0:T(8,128)(2,1)} %param.11), kind=kOutput, calls=%fused_computation.28 | convolution fusion | flops 3758096384 | bytes 19398656 | tf_op jit(solution)/shard_map/dot_general | solution.py:48
  31.1 3.4 pad_maximum_fusion
  34.6 0.0 reduce-scatter.2.cloned.1.call-update
  34.6 0.0 all-gather.8.cloned.1.call-start
  34.6 69.5 %all-reduce.9.cloned.1.call-done = (f32[256,2048]{1,0:T(8,128)}, f32[256,2048]{1,0:T(8,128)}) async-done(((f32[256,2048]{1,0:T(8,128)}, f32[256,2048]{1,0:T(8,128)}), (f32[256,2048]{1,0:T(8,128)}, f32[256,2048]{1,0:T(8,128)})) %all-reduce.9.cloned.1.call-update) | async-done | bytes 4194320 | tf_op jit(solution)/shard_map/psum | solution.py:22
  104.2 0.0 copy-start.5
  104.2 3.0 multiply_convert_fusion.3
  107.2 0.5 copy-done.5
  107.6 2.3 fusion.16
  109.9 0.0 all-gather.8.cloned.1.call-update
  109.9 0.0 all-gather.6.cloned.1.call-start
  110.0 54.5 %reduce-scatter.2.cloned.1.call-done = f32[64,7168]{1,0:T(8,128)} async-done(((f32[256,7168]{1,0:T(8,128)}), f32[64,7168]{1,0:T(8,128)}) %reduce-scatter.2.cloned.1.call-update) | async-done | bytes 1835024 | tf_op jit(solution)/shard_map/reduce_scatter | solution.py:30
  164.5 2.5 fusion.2
  167.0 0.0 all-gather.6.cloned.1.call-update
  167.0 0.0 all-reduce.5.cloned.1.call-start
  167.0 80.6 %all-gather.8.cloned.1.call-done = f32[1024,1024]{1,0:T(8,128)} async-done(((f32[256,1024]{1,0:T(8,128)}), f32[1024,1024]{1,0:T(8,128)}) %all-gather.8.cloned.1.call-update) | async-done | bytes 4194320 | tf_op jit(solution)/shard_map/all_gather | solution.py:26
  247.7 2.7 reduce_sum.18
  250.3 39.0 %all-gather.6.cloned.1.call-done = bf16[256,3584]{1,0:T(8,128)(2,1)} async-done(((bf16[64,3584]{1,0:T(8,128)(2,1)}), bf16[256,3584]{1,0:T(8,128)(2,1)}) %all-gather.6.cloned.1.call-update) | async-done | bytes 1835024 | tf_op jit(solution)/shard_map/all_gather | solution.py:39
  289.4 0.0 copy-start.2
  289.4 7.9 %fusion.19 = f32[256,2048]{1,0:T(8,128)S(1)} fusion(bf16[256,3584]{1,0:T(8,128)(2,1)} %all-gather.6.cloned.1.call-done, bf16[3584,2048]{1,0:T(8,128)(2,1)} %param.13), kind=kOutput, calls=%fused_computation.30 | convolution fusion | flops 3758096384 | bytes 18612224 | tf_op jit(solution)/shard_map/dot_general | solution.py:53
  297.3 0.0 copy-done.2
  297.3 2.6 convolution_subtract_fusion
  299.9 0.0 all-reduce.5.cloned.1.call-update
  300.0 0.2 all-gather.10.cloned.1.call-start
  300.2 50.1 %all-reduce.5.cloned.1.call-done = f32[256,2048]{1,0:T(8,128)} async-done(((f32[256,2048]{1,0:T(8,128)}), f32[256,2048]{1,0:T(8,128)}) %all-reduce.5.cloned.1.call-update) | async-done | bytes 2097168 | tf_op jit(solution)/shard_map/psum | solution.py:22
  350.3 5.1 fusion.3
  355.4 0.0 all-gather.10.cloned.1.call-update
  355.4 0.0 all-reduce.7.cloned.1.call-start
  355.5 80.7 %all-gather.10.cloned.1.call-done = f32[1024,1024]{1,0:T(8,128)} async-done(((f32[256,1024]{1,0:T(8,128)}), f32[1024,1024]{1,0:T(8,128)}) %all-gather.10.cloned.1.call-update) | async-done | bytes 4194320 | tf_op jit(solution)/shard_map/all_gather | solution.py:26
  436.2 2.7 reduce_sum.19
  438.9 4.8 fusion.20
  443.7 0.0 all-reduce.7.cloned.1.call-update
  443.7 4.9 convolution_convert_fusion
  448.6 3.3 convolution_convert_fusion.1
  451.9 41.8 %all-reduce.7.cloned.1.call-done = f32[256,2048]{1,0:T(8,128)} async-done(((f32[256,2048]{1,0:T(8,128)}), f32[256,2048]{1,0:T(8,128)}) %all-reduce.7.cloned.1.call-update) | async-done | bytes 2097168 | tf_op jit(solution)/shard_map/psum | solution.py:22
  493.7 7.0 %convert_bitcast_fusion.1 = bf16[1024,2048]{0,1:T(8,128)(2,1)} fusion(bf16[256,1024]{1,0:T(8,128)(2,1)S(1)} %copy-done.6, f32[256,2048]{1,0:T(8,128)} %get-tuple-element.8, f32[256,2048]{1,0:T(8,128)} %all-reduce.7.cloned.1.call-done, f32[256,2048]{1,0:T(8,128)} %get-tuple-element.9), kind=kOutput, calls=%fused_computation.2 | convolution fusion | flops 1081081856 | bytes 11010048 | tf_op jit(solution)/shard_map/dot_general | solution.py:10
  500.7 0.0 copy-start.3
  500.7 0.0 copy-start.7
  500.7 6.6 %copy.13 = bf16[1024,2048]{1,0:T(8,128)(2,1)} copy(bf16[1024,2048]{0,1:T(8,128)(2,1)} %convert_bitcast_fusion.1) | data formatting | bytes 8388608
  507.3 0.0 copy-done.3
  507.3 0.0 copy-done.7
  507.3 4.9 convert_bitcast_fusion
  512.2 0.0 copy-start.1
  512.2 6.5 %copy.14 = bf16[1024,2048]{1,0:T(8,128)(2,1)} copy(bf16[1024,2048]{0,1:T(8,128)(2,1)} %convert_bitcast_fusion) | data formatting | bytes 8388608
  518.8 0.0 copy-done.1
Async XLA Ops:
  8.0 7.8 %copy-start = (bf16[256,2048]{1,0:T(8,128)(2,1)S(1)}, bf16[256,2048]{1,0:T(8,128)(2,1)}, u32[]{:S(2)}) copy-start(bf16[256,2048]{1,0:T(8,128)(2,1)} %param.9) | copy-start | bytes 3145732
  8.0 5.1 copy-start.6
  8.0 96.2 %all-reduce.9.cloned.1.call-start = ((), (), s32[]{:S(2)}) async-start(), calls=%async_computation.7 | async-start | bytes 8388608 | tf_op jit(solution)/shard_map/psum | solution.py:22
  8.1 5.1 copy-start.4
  15.8 148.7 %reduce-scatter.2.cloned.1.call-start = ((), (), s32[]{:S(2)}) async-start(), calls=%async_computation.1 | async-start | bytes 9175040 | tf_op jit(solution)/shard_map/reduce_scatter | solution.py:30
  34.6 213.1 %all-gather.8.cloned.1.call-start = ((), (), s32[]{:S(2)}) async-start(), calls=%async_computation.5 | async-start | bytes 5242880 | tf_op jit(solution)/shard_map/all_gather | solution.py:26
  104.2 3.4 copy-start.5
  109.9 179.5 %all-gather.6.cloned.1.call-start = ((), (), s32[]{:S(2)}) async-start(), calls=%async_computation.2 | async-start | bytes 2293760 | tf_op jit(solution)/shard_map/all_gather | solution.py:39
  167.0 183.3 %all-reduce.5.cloned.1.call-start = ((), (), s32[]{:S(2)}) async-start(), calls=%async_computation.3 | async-start | bytes 4194304 | tf_op jit(solution)/shard_map/psum | solution.py:22
  289.4 7.9 %copy-start.2 = (bf16[1024,2048]{1,0:T(8,128)(2,1)S(1)}, bf16[1024,2048]{1,0:T(8,128)(2,1)}, u32[]{:S(2)}) copy-start(bf16[1024,2048]{1,0:T(8,128)(2,1)} %param.17) | copy-start | bytes 12582916
  300.0 136.2 %all-gather.10.cloned.1.call-start = ((), (), s32[]{:S(2)}) async-start(), calls=%async_computation.6 | async-start | bytes 5242880 | tf_op jit(solution)/shard_map/all_gather | solution.py:26
  355.4 138.3 %all-reduce.7.cloned.1.call-start = ((), (), s32[]{:S(2)}) async-start(), calls=%async_computation.4 | async-start | bytes 4194304 | tf_op jit(solution)/shard_map/psum | solution.py:22
  500.7 6.6 %copy-start.3 = (f32[256,2048]{1,0:T(8,128)S(1)}, f32[256,2048]{1,0:T(8,128)}, u32[]{:S(2)}) copy-start(f32[256,2048]{1,0:T(8,128)} %get-tuple-element.8) | copy-start | bytes 6291460
  500.7 6.6 %copy-start.7 = (bf16[256,1024]{1,0:T(8,128)(2,1)S(1)}, bf16[256,1024]{1,0:T(8,128)(2,1)}, u32[]{:S(2)}) copy-start(bf16[256,1024]{1,0:T(8,128)(2,1)} %param.10) | copy-start | bytes 1572868
  512.2 6.5 %copy-start.1 = (bf16[256,2048]{1,0:T(8,128)(2,1)S(1)}, bf16[256,2048]{1,0:T(8,128)(2,1)}, u32[]{:S(2)}) copy-start(bf16[256,2048]{1,0:T(8,128)(2,1)} %param.9) | copy-start | bytes 3145732
Sparse Core Ops, SparseCore 0:
  15.9 88.2 all-reduce.8
  300.1 50.1 all-reduce.4
  443.8 49.8 all-reduce.6
Sparse Core Ops, SparseCore 1:
  34.7 129.8 reduce-scatter.1
  166.5 81.1 all-gather.7
  249.7 39.7 all-gather.5
  355.5 80.6 all-gather.9
